TPU v7x, 256 devices: a whole 4x4x8 slice. The times are simulated.
256 devices in a mesh: grp: 4 (over y), col: 64 (over x, z, core).
Axes of the slice: x: 4, y: 4, z: 8, core: 2. Of those that a mesh axis runs over, the one named last changes fastest.
Arguments:
- inputs: bfloat16 [24, 256, 8192], P('grp', 'col'), may hold values from -6 to 6
- out_grads: bfloat16 [24, 256, 8192], P('grp', None, 'col'), may hold values from -0.5 to 0.5
- first_moment: float32 [8192, 8192], P(None, 'col'), may hold values from -2 to 2
- second_moment: float32 [8192, 8192], P(None, 'col'), may hold values from 0.01 to 1
- signs_in: int32 [8192], replicated, may hold values from 0 to 1
- signs_out: int32 [8192], replicated, may hold values from 0 to 1
- rows_in: int32 [64], replicated, may hold values from 0 to 8191, as said below
- rows_out: int32 [128], replicated, may hold values from 0 to 8191, as said below
- task_ids: int32 [24], P('grp'), may hold values from 0 to 7
- weights: int32 [24], P('grp'), may hold values from 1 to 4
Outputs:
- prototypes: float32 [8, 64, 128], P('grp', 'col')
Inputs may be any that keep to these rules, and one draw needn't show every extreme that they name: `rows_in`: distinct row numbers. `rows_out`: distinct row numbers.
All inputs are finite; a program needn't handle non-finite values.
Results may differ from a plain program's by a relative error of at most 0.0019.
Values may be sent and summed in bfloat16 or wider, within the bound.
A program may use at most 128 MiB of HBM per device.

v0:
```python
import math

import jax
import jax.numpy as jnp
from jax import lax
from jax.sharding import PartitionSpec as P

PRO_GRP = 2


def hadamard_rows(rows, sign_bits, cols, width):
    both = jnp.bitwise_and(rows[:, None], cols[None, :])
    parity = jnp.zeros(both.shape, jnp.int32)
    for bit in range(int(math.log2(width)) + 1):
        parity = jnp.bitwise_xor(parity, jnp.bitwise_and(jnp.right_shift(both, bit), 1))
    value = (1 - 2 * parity) * (1 - 2 * sign_bits)[None, :]
    return value.astype(jnp.float32)


def body(
    inputs,
    out_grads,
    first_moment,
    second_moment,
    signs_in,
    signs_out,
    rows_in,
    rows_out,
    task_ids,
    weights,
):
    width = first_moment.shape[0]
    n_col = lax.axis_size("col")
    n_grp = lax.axis_size("grp")
    grad = jnp.einsum(
        "etd,etc->edc",
        lax.all_gather(inputs, "col", axis=1, tiled=True),
        out_grads,
        preferred_element_type=jnp.float32,
    )
    first = 0.9 * first_moment[None] + 0.1 * grad
    second = 0.999 * second_moment[None] + 0.001 * grad * grad
    update = (first / (jnp.sqrt(second) + 1e-08)).astype(jnp.bfloat16)
    all_cols = jnp.arange(width, dtype=jnp.int32)
    left = hadamard_rows(rows_in, signs_in, all_cols, width).astype(jnp.bfloat16)
    half = jnp.einsum("rd,edc->erc", left, update, preferred_element_type=jnp.float32)
    right = hadamard_rows(rows_out, signs_out, all_cols, width)
    owned = lax.all_to_all(half, "col", split_axis=1, concat_axis=2, tiled=True)
    sketch = jnp.einsum("erd,kd->erk", owned, right, precision=lax.Precision.HIGHEST)
    entries = sketch.shape[1] * n_col * sketch.shape[2]
    squares = lax.psum(jnp.sum(sketch * sketch, axis=(1, 2)), "col")
    unit = sketch * lax.rsqrt(squares / entries + 1e-06)[:, None, None]
    n_proto = PRO_GRP * n_grp
    protos = jnp.arange(n_proto, dtype=jnp.int32)
    coef = jnp.where(
        task_ids[:, None] == protos[None, :], weights[:, None].astype(jnp.float32), jnp.float32(0.0)
    )
    term = jnp.einsum("ep,erk->prk", coef, unit, precision=lax.Precision.HIGHEST)
    return lax.psum_scatter(term, "grp", scatter_dimension=0, tiled=True)


def solution(mesh):
    placed = (
        P("grp", "col", None),
        P("grp", None, "col"),
        P(None, "col"),
        P(None, "col"),
        P(),
        P(),
        P(),
        P(),
        P("grp"),
        P("grp"),
    )
    return jax.shard_map(
        body, mesh=mesh, in_specs=placed, out_specs=P("grp", "col", None), check_vma=False
    )
```

profile of v0, /device:TPU:1, one launch (start us, length us, event | category | flops | bytes accessed | tf_op | source)
XLA Modules:
  0.0 380.8 jit_solution(12265177928836386276)
XLA Ops:
  6.5 0.0 copy-start
  6.5 0.0 all-gather.2.cloned.1.call-start
  6.5 2.1 copy.12
  8.6 0.0 all-gather.2.cloned.1.call-update
  8.6 0.8 multiply_subtract_fusion.1
  9.4 0.0 copy-start.2
  9.4 7.4 %broadcast_multiply_fusion = (f32[8192,128]{1,0:T(8,128)}, f32[8192,128]{1,0:T(8,128)}) fusion(f32[8192,128]{1,0:T(8,128)} %param.13, f32[8192,128]{1,0:T(8,128)} %param.12), kind=kLoop, calls=%fused_computation.74 | loop fusion | flops 2097152 | bytes 16777216 | tf_op jit(solution)/shard_map/mul | solution.py:42
  16.8 139.2 %all-gather.2.cloned.1.call-done = bf16[6,256,8192]{2,0,1:T(8,128)(2,1)} async-done(((bf16[6,4,8192]{2,0,1:T(8,128)(2,1)}), bf16[6,256,8192]{2,0,1:T(8,128)(2,1)}) %all-gather.2.cloned.1.call-update) | async-done | bytes 25165840 | tf_op jit(solution)/shard_map/all_gather | solution.py:37
  156.0 0.0 copy-done
  156.0 0.0 copy-done.2
  156.0 0.0 copy-start.3
  156.0 0.0 copy-start.6
  156.0 0.0 copy-start.1
  156.0 0.0 copy-start.4
  156.1 56.8 %fusion.76 = f32[6,64,128]{2,1,0:T(8,128)S(1)} fusion(bf16[6,256,128]{2,1,0:T(8,128)(2,1)S(1)} %copy-done, bf16[6,256,8192]{2,0,1:T(8,128)(2,1)} %all-gather.2.cloned.1.call-done, f32[8192,128]{1,0:T(8,128)} %get-tuple-element.7, f32[8192,128]{1,0:T(8,128)} %get-tuple-element.8, s32[8192]{0:T(1024)S(1)} %multiply_subtract_fusion.1, s32[64]{0:T(128)S(1)} %copy-done.2), kind=kOutput, calls=%fused_computation.76 | convolution fusion | flops 4101505024 | bytes 34177280 | tf_op jit(solution)/shard_map/rd,edc->erc/dot_general | solution.py:46
  212.8 0.8 copy.14
  213.6 6.0 %all-to-all-start = ((f32[6,64,128]{2,0,1:T(8,128)}), f32[6,64,128]{2,0,1:T(8,128)S(1)}, u32[]{:S(2)}, u32[]{:S(2)}) async-start(f32[6,64,128]{2,0,1:T(8,128)} %copy.14), calls=%async_computation | async-start | bytes 524288 | tf_op jit(solution)/shard_map/all_to_all | solution.py:48
  219.6 0.0 copy-done.3
  219.6 0.0 copy-done.6
  219.6 0.6 dynamic-slice
  220.9 0.0 copy-done.1
  220.9 0.0 copy-start.5
  220.9 10.6 %all-to-all-done = f32[6,64,128]{2,0,1:T(8,128)S(1)} async-done(((f32[6,64,128]{2,0,1:T(8,128)}), f32[6,64,128]{2,0,1:T(8,128)S(1)}, u32[]{:S(2)}, u32[]{:S(2)}) %all-to-all-start) | async-done | bytes 196640 | tf_op jit(solution)/shard_map/all_to_all | solution.py:48
  231.6 0.0 copy-done.4
  231.6 9.2 %multiply_reduce_fusion = (f32[6]{0:T(128)S(1)}, f32[6,128]{1,0:T(8,128)S(1)}) fusion(s32[8192]{0:T(1024)S(1)} %multiply_subtract_fusion, s32[128]{0:T(128)S(1)} %copy-done.4, f32[6,64,128]{2,0,1:T(8,128)S(1)} %all-to-all-done), kind=kOutput, calls=%fused_computation.99 | convolution fusion | flops 123733496 | bytes 232984 | tf_op jit(solution)/shard_map/erd,kd->erk/dot_general | solution.py:49
  240.8 123.9 %psum.7 = f32[6]{0:T(128)S(1)} all-reduce(f32[6]{0:T(128)S(1)} %get-tuple-element.5), channel_id=1, replica_groups=mesh['grp'=4,'col'=64] {'col'}, use_global_device_ids=true, to_apply=%region_1.0 | all-reduce | flops 6 | bytes 48 | tf_op jit(solution)/shard_map/psum | solution.py:51
  364.6 0.0 copy-done.5
  364.6 0.3 convolution_bitcast_fusion
  364.9 8.4 %all-reduce = f32[8,1,128]{2,0,1:T(8,128)S(1)} all-reduce(f32[8,1,128]{2,0,1:T(8,128)S(1)} %convolution_bitcast_fusion), channel_id=2, replica_groups=mesh['grp'=4,'col'=64] {'grp'}, use_global_device_ids=true, to_apply=%region_2.3.clone | all-reduce | flops 1024 | bytes 8192
  373.3 0.6 constant_dynamic-slice_fusion
  (3 shorter events, 0.0 us)
Async XLA Ops:
  6.5 149.5 %copy-start = (bf16[6,256,128]{2,1,0:T(8,128)(2,1)S(1)}, bf16[6,256,128]{2,1,0:T(8,128)(2,1)}, u32[]{:S(2)}) copy-start(bf16[6,256,128]{2,1,0:T(8,128)(2,1)} %param.11) | copy-start | bytes 1179652
  6.5 149.5 %all-gather.2.cloned.1.call-start = ((), (), s32[]{:S(2)}) async-start(), calls=%async_computation.1 | async-start | bytes 34078720 | tf_op jit(solution)/shard_map/all_gather | solution.py:37
  9.4 146.6 %copy-start.2 = (s32[64]{0:T(128)S(1)}, s32[64]{0:T(128)}, u32[]{:S(2)}) copy-start(s32[64]{0:T(128)} %param.16) | copy-start | bytes 772
  156.0 63.6 %copy-start.3 = (s32[6]{0:T(128)S(1)}, s32[6]{0:T(128)}, u32[]{:S(2)}) copy-start(s32[6]{0:T(128)} %param.19) | copy-start | bytes 76
  156.0 63.6 %copy-start.6 = (u32[256]{0:T(256)S(1)}, u32[256]{0:T(256)}, u32[]{:S(2)}) copy-start(u32[256]{0:T(256)} %constant.13) | copy-start | bytes 3076
  156.0 64.9 %copy-start.1 = (s32[8192]{0:T(1024)S(1)}, s32[8192]{0:T(1024)}, u32[]{:S(2)}) copy-start(s32[8192]{0:T(1024)} %param.15) | copy-start | bytes 98308
  156.0 75.5 %copy-start.4 = (s32[128]{0:T(128)S(1)}, s32[128]{0:T(128)}, u32[]{:S(2)}) copy-start(s32[128]{0:T(128)} %param.17) | copy-start | bytes 1540
  213.6 17.9 %all-to-all-start = ((f32[6,64,128]{2,0,1:T(8,128)}), f32[6,64,128]{2,0,1:T(8,128)S(1)}, u32[]{:S(2)}, u32[]{:S(2)}) async-start(f32[6,64,128]{2,0,1:T(8,128)} %copy.14), calls=%async_computation | async-start | bytes 524288 | tf_op jit(solution)/shard_map/all_to_all | solution.py:48
  220.9 143.7 %copy-start.5 = (s32[6]{0:T(128)S(1)}, s32[6]{0:T(128)}, u32[]{:S(2)}) copy-start(s32[6]{0:T(128)} %param.18) | copy-start | bytes 76
Sparse Core Ops, SparseCore 0:
  10.1 145.8 all-gather.1
where the time goes:
time: 382 us; the launch traced here: 381 us
  waiting for transfers between devices  150 us (39%)
  blocking collectives  132 us (35%)
  matrix products  66.2 us (17%)
  between operations  14.2 us (4%)
  other arithmetic  8.18 us (2%)
  starting transfers between devices  5.96 us (2%)
  local copies, waits for them, and re-layouts  4.09 us (1%)
    all_gather x1, waiting for transfers between devices, body(): lax.all_gather(inputs, 'col', axis=1, tiled=True)  139 us
    psum x1, blocking collectives, body(): squares = lax.psum(jnp.sum(sketch * sketch, axis=(1, 2)), 'col')  124 us
    dot_general x1, matrix products, body(): jnp.einsum('rd,edc->erc', left, update, preferred_element_type=jnp.float32)  56.8 us
    all_to_all x1, waiting for transfers between devices, body(): owned = lax.all_to_all(half, 'col', split_axis=1, concat_axis=2, tiled=True)  10.6 us
    dot_general x1, matrix products, body(): jnp.einsum('erd,kd->erk', owned, right, precision=lax.Precision.HIGHEST)  9.18 us
    unnamed x1, blocking collectives  8.44 us
  transfers between devices with their start and end apart: 2, of which 2 were waited for; matrix products, arithmetic and copies ran while one was open for 2% of the time, Pallas kernels for 0%

commit v1 on v0

v1 whole, which is shorter than its diff:
```python
import functools
import math

import jax
import jax.numpy as jnp
from jax import lax
from jax.experimental import pallas as pl
from jax.experimental.pallas import tpu as pltpu
from jax.sharding import PartitionSpec as P

MESH = pl.DeviceIdType.MESH
F32 = jnp.float32
BF16 = jnp.bfloat16

NY = 4
NX = 4
NZ = 8
NCOL = NX * NZ * 2
EX = 6
EA = 3
TK = 4
D = 8192
QD = D // 4
CH = 256
NCH = QD // CH
SUB = CH // NY
C = 128
R1 = 64
R2 = 128
HALF = 128
PRO = 2

K_FM = 9.0 * math.sqrt(10.0)
K_G = math.sqrt(10.0)
K_SM = 999.0
K_EPS = 1e-8 * math.sqrt(1000.0)


def parity(both):
    for shift in (8, 4, 2, 1):
        both = jnp.bitwise_xor(both, jnp.right_shift(both, shift))
    return jnp.bitwise_and(both, 1)


def as_column(row, height):
    width = row.shape[1]
    r = lax.broadcasted_iota(jnp.int32, (height, width), 0)
    c = lax.broadcasted_iota(jnp.int32, (height, width), 1)
    return jnp.sum(jnp.where(r == c, jnp.broadcast_to(row, (height, width)), 0.0), axis=1, keepdims=True)


def as_row(column, width):
    height = column.shape[0]
    r = lax.broadcasted_iota(jnp.int32, (height, width), 0)
    c = lax.broadcasted_iota(jnp.int32, (height, width), 1)
    return jnp.sum(jnp.where(r == c, jnp.broadcast_to(column, (height, width)), 0.0), axis=0, keepdims=True)


def kernel(
    x_ref, og_ref, fm_ref, sm_ref, sin_ref, sout_ref, rin_ref, rout_ref, tid_ref, w_ref,
    out_ref,
    rx, xs, xg, ogb, ogt, fmb, smb, ta, tb, left_s, right_s, hacc, sk, rs, qs, qr, ts, yr,
    s_rx, s_rxs, s_ogl, s_og, s_ogs, s_ml, s_mc, s_mcs, s_mx, s_mxs, s_my, s_mys,
    s_ax, s_axs, s_az, s_azs, s_bz, s_bzs, s_bx, s_bxs,
    s_rs, s_rss, s_q, s_qs, s_t, s_tss,
):
    y = lax.axis_index("grp")
    me = lax.axis_index("col")
    core = lax.rem(me, 2)
    z = lax.rem(me // 2, NZ)
    x = me // (2 * NZ)
    pair = x // 2
    low = lax.rem(x, 2)
    cls = lax.rem(pair + low, 2)
    quarter = 2 * cls + core
    blk = 2 * low + core

    def col(x_, z_, c_):
        return (x_ * NZ + z_) * 2 + c_

    xpart = x + 1 - 2 * low
    cross = NX - 1 - x
    zp = lax.rem(z + 1, NZ)
    zm = lax.rem(z + NZ - 1, NZ)
    yp = lax.rem(y + 1, NY)
    ym = lax.rem(y + NY - 1, NY)
    d_core = (y, col(x, z, 1 - core))
    d_xp = tuple((y, col(xpart, z, c_)) for c_ in range(2))
    d_xsame = (y, col(xpart, z, core))
    d_cross = (y, col(cross, z, core))
    d_z = ((y, col(x, zp, core)), (y, col(x, zm, core)))
    d_y = ((yp, me), (ym, me))

    def remote(src, dst, ssem, rsem, dev):
        return pltpu.make_async_remote_copy(
            src_ref=src, dst_ref=dst, send_sem=ssem, recv_sem=rsem, device_id=dev, device_id_type=MESH
        )

    barrier = pltpu.get_barrier_semaphore()

    @pl.loop(1, NCOL)
    def _(k):
        pl.semaphore_signal(barrier, inc=1, device_id=(y, lax.rem(me + k, NCOL)), device_id_type=MESH)

    for k in range(1, NY):
        pl.semaphore_signal(barrier, inc=1, device_id=(lax.rem(y + k, NY), me), device_id_type=MESH)

    og_local = []
    for p_ in range(2):
        for l_ in range(2):
            cp = pltpu.make_async_copy(og_ref.at[:, p_, l_], ogb.at[blk, :, p_, :, l_], s_ogl.at[2 * p_ + l_])
            cp.start()
            og_local.append(cp)
    x_local = pltpu.make_async_copy(x_ref.at[:, :, pl.ds(pl.multiple_of(quarter * QD, QD), QD)], rx.at[blk], s_rx.at[blk])
    x_local.start()
    pl.semaphore_wait(barrier, NCOL - 1 + NY - 1)

    def x_send(dev, q, i):
        return remote(x_ref.at[:, :, pl.ds(pl.multiple_of(q * QD, QD), QD)], rx.at[blk], s_rxs.at[i], s_rx.at[blk], dev)

    x_sends = [
        x_send(d_xp[0], 2 * (1 - cls), 0),
        x_send(d_xp[1], 2 * (1 - cls) + 1, 1),
        x_send(d_core, 2 * cls + 1 - core, 2),
    ]
    for cp in x_sends:
        cp.start()
    for cp in og_local:
        cp.wait()
    og_core = remote(ogb.at[blk], ogb.at[blk], s_ogs.at[0], s_og.at[0], d_core)
    og_xp = remote(ogb.at[blk], ogb.at[blk], s_ogs.at[1], s_og.at[1], d_xsame)
    og_xp.start()
    og_core.start()

    rows_in = as_column(rin_ref[...].astype(F32), R1).astype(jnp.int32)
    rows_out = as_column(rout_ref[...].astype(F32), R2).astype(jnp.int32)

    @pl.loop(0, NCH)
    def _(j):
        tile = quarter * NCH + j
        cols = lax.broadcasted_iota(jnp.int32, (R1, CH), 1) + tile * CH
        bit = jnp.bitwise_xor(parity(jnp.bitwise_and(rows_in, cols)), jnp.broadcast_to(sin_ref[tile], (R1, CH)))
        left_s[j] = (1 - 2 * bit).astype(F32).astype(BF16)

    for b in range(4):
        owner = col(2 * pair + b // 2, z, b % 2)
        cols = lax.broadcasted_iota(jnp.int32, (R2, C), 1) + owner * C
        bit = jnp.bitwise_xor(parity(jnp.bitwise_and(rows_out, cols)), jnp.broadcast_to(sout_ref[owner], (R2, C)))
        right_s[:, b * C:(b + 1) * C] = (1 - 2 * bit).astype(F32).astype(BF16)

    hacc[...] = jnp.zeros_like(hacc)
    sk[...] = jnp.zeros_like(sk)

    for b in range(4):
        pltpu.make_async_copy(rx.at[b], rx.at[b], s_rx.at[b]).wait()
        xs[:, TK * b:TK * (b + 1), :] = rx[b].astype(F32)

    for j in range(NCH):
        xg[j, :, pair, z] = xs[:, :, j * CH:(j + 1) * CH].astype(BF16)

    A = slice(0, EA)
    B = slice(EA, EX)

    def zback(s, up):
        return lax.rem(z + NZ - (s - 1), NZ) if up == 0 else lax.rem(z + s - 1, NZ)

    def zcome(s, up):
        return lax.rem(z + NZ - s, NZ) if up == 0 else lax.rem(z + s, NZ)

    def a_x(j, where):
        v = xg.at[j, A, where, z]
        return remote(v, v, s_axs.at[j], s_ax.at[j], d_cross)

    def a_z(j, s, up, zz):
        v = xg.at[j, A, :, zz] if s < 4 else xg.at[j, A, :, zz, :, pl.ds(up * HALF, HALF)]
        return remote(v, v, s_azs.at[j, up, s - 1], s_az.at[j, up, s - 1], d_z[up])

    def b_z(j, s, up, zz):
        v = xg.at[j, B, pair, zz] if s < 4 else xg.at[j, B, pair, zz, :, pl.ds(up * HALF, HALF)]
        return remote(v, v, s_bzs.at[j, up, s - 1], s_bz.at[j, up, s - 1], d_z[up])

    def b_x(j, where):
        v = xg.at[j, B, where]
        return remote(v, v, s_bxs.at[j], s_bx.at[j], d_cross)

    moments = ((fm_ref, fmb), (sm_ref, smb))

    def rows(q, j, extra, n):
        return pl.ds(pl.multiple_of(q * QD + j * CH + extra, SUB), n)

    def m_local(j, a):
        return pltpu.make_async_copy(moments[a][0].at[rows(quarter, j, 0, CH)], moments[a][1].at[j, blk], s_ml.at[j, a])

    def m_core(j, a, b):
        q = 2 * cls + 1 - core
        return remote(moments[a][0].at[rows(q, j, 0, CH)], moments[a][1].at[j, b], s_mcs.at[j, a], s_mc.at[j, a], d_core)

    def m_x(j, a, h):
        q = 2 * (1 - cls) + h
        return remote(
            moments[a][0].at[rows(q, j, y * SUB, SUB)],
            moments[a][1].at[j, blk, pl.ds(pl.multiple_of(y * SUB, SUB), SUB)],
            s_mxs.at[j, a, h], s_mx.at[j, a, core], d_xp[h],
        )

    def m_x_come(j, a, h):
        v = moments[a][1].at[j, 2 * (1 - low) + h, pl.ds(pl.multiple_of(y * SUB, SUB), SUB)]
        return remote(v, v, s_mxs.at[j, a, h], s_mx.at[j, a, h], d_xp[h])

    def m_y(j, a, k, yy, up):
        v = moments[a][1].at[j, pl.ds(2 * (1 - low), 2), pl.ds(pl.multiple_of(yy * SUB, SUB), SUB)]
        return remote(v, v, s_mys.at[j, a, k], s_my.at[j, a, k], d_y[up])

    y2 = lax.rem(y + 2, NY)

    def stage(t, k, body):
        j = t - k

        @pl.when(jnp.logical_and(j >= 0, j < NCH))
        def _():
            body(j)

    def st5(j):
        for up in range(2):
            a_z(j, 4, up, zcome(4, up)).wait_recv()
        b_x(j, 1 - pair).wait_recv()

    def st4(j):
        for up in range(2):
            b_z(j, 4, up, zcome(4, up)).wait_recv()
        b_x(j, pair).start()
        for up in range(2):
            a_z(j, 3, up, zcome(3, up)).wait_recv()
            a_z(j, 4, up, zback(4, up)).start()

    def st3(j):
        for up in range(2):
            b_z(j, 3, up, zcome(3, up)).wait_recv()
            b_z(j, 4, up, zback(4, up)).start()
        for up in range(2):
            a_z(j, 2, up, zcome(2, up)).wait_recv()
            a_z(j, 3, up, zback(3, up)).start()

    def st2(j):
        for up in range(2):
            b_z(j, 2, up, zcome(2, up)).wait_recv()
            b_z(j, 3, up, zback(3, up)).start()
        for up in range(2):
            a_z(j, 1, up, zcome(1, up)).wait_recv()
            a_z(j, 2, up, zback(2, up)).start()
        m_y(j, 0, 0, ym, 0).wait_recv()
        m_y(j, 0, 2, ym, 0).start()
        m_y(j, 1, 1, yp, 1).wait_recv()
        m_y(j, 1, 2, yp, 1).start()

    def st1(j):
        for up in range(2):
            b_z(j, 1, up, zcome(1, up)).wait_recv()
            b_z(j, 2, up, zback(2, up)).start()
        a_x(j, 1 - pair).wait_recv()
        for up in range(2):
            a_z(j, 1, up, zback(1, up)).start()
        for a in range(2):
            for h in range(2):
                m_x_come(j, a, h).wait_recv()
            for up in range(2):
                m_y(j, a, up, y, up).start()

    def st0(j):
        a_x(j, pair).start()
        for up in range(2):
            b_z(j, 1, up, zback(1, up)).start()
        for a in range(2):
            for h in range(2):
                m_x(j, a, h).start()
        for a in range(2):
            m_core(j, a, blk).start()
            m_local(j, a).start()

    def compute(j):
        for a in range(2):
            m_y(j, a, 1 - a, (yp, ym)[a], 1 - a).wait_recv()
            m_y(j, a, 2, y2, a).wait_recv()
            m_core(j, a, 2 * low + 1 - core).wait_recv()
            m_local(j, a).wait()
        for b in range(4):
            ta[b * C:(b + 1) * C, :] = (fmb[j, b] * K_FM).T
            tb[b * C:(b + 1) * C, :] = (smb[j, b] * K_SM).T

        @pl.loop(0, EX)
        def _(e):
            acts = xg[j, e].reshape(2 * NZ * 4 * TK, CH)
            for h in range(2):
                sl = slice(h * 2 * C, (h + 1) * 2 * C)
                g = jnp.dot(ogt[e, sl, :], acts, preferred_element_type=F32)
                v = g * g + tb[sl, :]
                m = g * K_G + ta[sl, :]
                u = (m / (v * lax.rsqrt(v) + K_EPS)).astype(BF16)
                hacc[e, :, sl] += lax.dot_general(
                    left_s[j], u, (((1,), (1,)), ((), ())), preferred_element_type=F32
                )

    def og_forward():
        og_in = remote(ogb.at[2 * (1 - low) + core], ogb.at[2 * (1 - low) + core], s_ogs.at[1], s_og.at[1], d_xsame)
        og_in.wait_recv()
        remote(ogb.at[2 * (1 - low) + core], ogb.at[2 * (1 - low) + core], s_ogs.at[2], s_og.at[2], d_core).start()

    def og_finish():
        b1 = 2 * low + 1 - core
        b2 = 2 * (1 - low) + 1 - core
        remote(ogb.at[b1], ogb.at[b1], s_ogs.at[0], s_og.at[0], d_core).wait_recv()
        remote(ogb.at[b2], ogb.at[b2], s_ogs.at[2], s_og.at[2], d_core).wait_recv()

        @pl.loop(0, EX)
        def _(e):
            for b in range(4):
                v = ogb[b, e].astype(F32).reshape(4 * NZ * 8, C)
                ogt[e, b * C:(b + 1) * C, :] = v.T.astype(BF16)

    @pl.loop(0, NCH + 5)
    def _(t):
        stage(t, 5, st5)
        stage(t, 4, st4)
        stage(t, 3, st3)
        stage(t, 2, st2)
        stage(t, 1, st1)
        stage(t, 0, st0)

        @pl.when(t == 2)
        def _():
            og_forward()

        @pl.when(t == 4)
        def _():
            og_finish()

        stage(t, 5, compute)

    for e in range(EX):
        h = hacc[e]
        hi = h.astype(BF16)
        rest = h - hi.astype(F32)
        mid = rest.astype(BF16)
        lo = (rest - mid.astype(F32)).astype(BF16)
        dims = (((1,), (1,)), ((), ()))
        part = lax.dot_general(lo, right_s[...], dims, preferred_element_type=F32)
        part = part + lax.dot_general(mid, right_s[...], dims, preferred_element_type=F32)
        part = part + lax.dot_general(hi, right_s[...], dims, preferred_element_type=F32)
        sk[:, e, :] = part

    @pl.loop(1, NCOL)
    def _(k):
        to = lax.rem(me + k, NCOL)
        remote(sk.at[to], rs.at[me], s_rss, s_rs, (y, to)).start()

    rs[me] = sk[me]
    some = rs.at[pl.ds(0, NCOL - 1)]
    remote(some, some, s_rss, s_rs, d_core).wait_recv()
    rows_sum = jnp.sum(rs[...], axis=0)

    sq = as_row(jnp.sum(rows_sum * rows_sum, axis=1, keepdims=True), C)
    qs[...] = sq

    @pl.loop(1, NCOL)
    def _(k):
        to = lax.rem(me + k, NCOL)
        remote(qs, qr.at[me], s_qs, s_q, (y, to)).start()

    qr[me] = sq
    someq = qr.at[pl.ds(0, NCOL - 1)]
    remote(someq, someq, s_qs, s_q, d_core).wait_recv()
    squares = as_column(jnp.sum(qr[...], axis=0), 8)
    unit = rows_sum * lax.rsqrt(squares / (R1 * R2) + 1e-06)

    tid = as_column(tid_ref[...].astype(F32), 8)
    wgt = as_column(w_ref[...].astype(F32), 8)

    def term(p):
        coef = jnp.where(tid == p.astype(F32), wgt, 0.0)
        return jnp.sum(coef * unit, axis=0, keepdims=True)

    def terms(g):
        return jnp.concatenate([term(PRO * g + i) for i in range(PRO)], axis=0)

    y_sends = []
    for k in range(1, NY):
        g = lax.rem(y + k, NY)
        ts[k - 1] = terms(g)
        cp = remote(ts.at[k - 1], yr.at[k - 1], s_tss.at[k - 1], s_t.at[k - 1], (g, me))
        cp.start()
        y_sends.append(cp)
    total = terms(y)
    for cp in y_sends:
        cp.wait()
    out_ref[...] = total + (yr[0] + yr[1] + yr[2])

    remote(some, some, s_rss, s_rs, d_core).wait_send()
    remote(someq, someq, s_qs, s_q, d_core).wait_send()
    for cp in x_sends:
        cp.wait_send()
    og_core.wait_send()
    og_xp.wait_send()
    remote(ogb.at[2 * (1 - low) + core], ogb.at[2 * (1 - low) + core], s_ogs.at[2], s_og.at[2], d_core).wait_send()

    @pl.loop(0, NCH)
    def _(j):
        a_x(j, pair).wait_send()
        b_x(j, pair).wait_send()
        for up in range(2):
            for s in range(1, 5):
                a_z(j, s, up, zback(s, up)).wait_send()
                b_z(j, s, up, zback(s, up)).wait_send()
        for a in range(2):
            m_core(j, a, blk).wait_send()
            for h in range(2):
                m_x(j, a, h).wait_send()
            for up in range(2):
                m_y(j, a, up, y, up).wait_send()
        m_y(j, 0, 2, ym, 0).wait_send()
        m_y(j, 1, 2, yp, 1).wait_send()


def body(
    inputs,
    out_grads,
    first_moment,
    second_moment,
    signs_in,
    signs_out,
    rows_in,
    rows_out,
    task_ids,
    weights,
):
    hbm = pl.BlockSpec(memory_space=pl.ANY)
    vmem = pl.BlockSpec(memory_space=pltpu.VMEM)
    dma = pltpu.SemaphoreType.DMA
    out = pl.pallas_call(
        kernel,
        out_shape=jax.ShapeDtypeStruct((PRO, C), F32),
        in_specs=[hbm] * 4 + [vmem] * 6,
        out_specs=vmem,
        scratch_shapes=[
            pltpu.VMEM((4, EX, TK, QD), BF16),
            pltpu.VMEM((EX, 4 * TK, QD), F32),
            pltpu.VMEM((NCH, EX, 2, NZ, 4 * TK, CH), BF16),
            pltpu.VMEM((4, EX, 2, NZ, 2, 8, C), BF16),
            pltpu.VMEM((EX, 4 * C, 256), BF16),
            pltpu.VMEM((NCH, 4, CH, C), F32),
            pltpu.VMEM((NCH, 4, CH, C), F32),
            pltpu.VMEM((4 * C, CH), F32),
            pltpu.VMEM((4 * C, CH), F32),
            pltpu.VMEM((NCH, R1, CH), BF16),
            pltpu.VMEM((R2, 4 * C), BF16),
            pltpu.VMEM((EX, R1, 4 * C), F32),
            pltpu.VMEM((NCOL, 8, C), F32),
            pltpu.VMEM((NCOL, 8, C), F32),
            pltpu.VMEM((1, C), F32),
            pltpu.VMEM((NCOL, 1, C), F32),
            pltpu.VMEM((NY - 1, PRO, C), F32),
            pltpu.VMEM((NY - 1, PRO, C), F32),
            dma((4,)), dma((3,)),
            dma((4,)), dma((3,)), dma((3,)),
            dma((NCH, 2)),
            dma((NCH, 2)), dma((NCH, 2)),
            dma((NCH, 2, 2)), dma((NCH, 2, 2)),
            dma((NCH, 2, 3)), dma((NCH, 2, 3)),
            dma((NCH,)), dma((NCH,)),
            dma((NCH, 2, 4)), dma((NCH, 2, 4)),
            dma((NCH, 2, 4)), dma((NCH, 2, 4)),
            dma((NCH,)), dma((NCH,)),
            dma, dma, dma, dma,
            dma((NY - 1,)), dma((NY - 1,)),
        ],
        compiler_params=pltpu.CompilerParams(
            collective_id=0, has_side_effects=True, vmem_limit_bytes=60 * 1024 * 1024
        ),
    )(
        inputs,
        out_grads.reshape(EX, 2, 2, NZ, 8, C),
        first_moment,
        second_moment,
        signs_in.reshape(D // CH, 1, CH),
        signs_out.reshape(NCOL, 1, C),
        rows_in.reshape(1, R1),
        rows_out.reshape(1, R2),
        task_ids.reshape(1, EX),
        weights.reshape(1, EX),
    )
    return out.reshape(PRO, 1, C)


def solution(mesh):
    placed = (
        P("grp", "col", None),
        P("grp", None, "col"),
        P(None, "col"),
        P(None, "col"),
        P(),
        P(),
        P(),
        P(),
        P("grp"),
        P("grp"),
    )
    return jax.shard_map(
        body, mesh=mesh, in_specs=placed, out_specs=P("grp", "col", None), check_vma=False
    )
```

time: 382 us -> 119 us (0.31)
  waiting for transfers between devices: 150 us -> 0 us
  blocking collectives: 132 us -> 0 us
  Pallas kernels: 0 us -> 117 us
  matrix products: 66.2 us -> 0 us
  between operations: 14.2 us -> 0.01 us
  other arithmetic: 8.18 us -> 0 us
  starting transfers between devices: 5.96 us -> 0 us
    all_gather x1 -> x0, waiting for transfers between devices: 139 us -> none  [body(): lax.all_gather(inputs, 'col', axis=1, tiled=True)]
    psum x1 -> x0, blocking collectives: 124 us -> none  [body(): squares = lax.psum(jnp.sum(sketch * sketch, axis=(1, 2)), 'col')]
    pallas_call x0 -> x1, Pallas kernels: none -> 117 us  [body(): pl.pallas_call(kernel, out_shape=jax.ShapeDtypeStruct((PRO, C), F32), in_...]
    dot_general x3 -> x0, matrix products: 66.2 us -> none  [the longest x1 56.8 us: body(): jnp.einsum('rd,edc->erc', left, update, preferred_element_type=jnp.float32)]
    all_to_all x1 -> x0, waiting for transfers between devices: 10.6 us -> none  [body(): owned = lax.all_to_all(half, 'col', split_axis=1, concat_axis=2, tiled=True)]
    unnamed x1 -> x0, blocking collectives: 8.44 us -> none
    mul x1 -> x0, other arithmetic: 7.4 us -> none  [body(): second = 0.999 * second_moment[None] + 0.001 * grad * grad]
    all_to_all x1 -> x0, starting transfers between devices: 5.95 us -> none  [body(): owned = lax.all_to_all(half, 'col', split_axis=1, concat_axis=2, tiled=True)]
  transfers between devices with their start and end apart: 2 -> 0, of which waited for: 2 -> 0; matrix products, arithmetic and copies ran while one was open for 2% -> 0% of each run, Pallas kernels for 0% -> 0%
where the time goes in v1:
time: 119 us
  Pallas kernels  117 us (98%)
  local copies, waits for them, and re-layouts  1.24 us (1%)
    pallas_call x1, Pallas kernels, body(): pl.pallas_call(kernel, out_shape=jax.ShapeDtypeStruct((PRO, C), F32), in_...  117 us

profile of v1, /device:TPU:1, one launch (start us, length us, event | category | flops | bytes accessed | tf_op | source)
XLA Modules:
  0.0 118.7 jit_solution(1797674702355935400)
XLA Ops:
  0.0 117.5 %shard_map.100 = f32[2,128]{1,0:T(2,128)} custom-call(bf16[6,4,8192]{2,1,0:T(4,128)(2,1)} %x_ref.1, bf16[6,2,2,8,8,128]{5,4,3,2,1,0:T(8,128)(2,1)} %bitcast.10, f32[8192,128]{1,0:T(8,128)} %fm_ref.1, f32[8192,128]{1,0:T(8,128)} %sm_ref.1, s32[32,1,256]{2,1,0:T(1,128)} %bitcast.11, s32[64,1,128]{2,1,0:T(1,128)} %bitcast.12, s32[1,64]{1,0:T(1,128)} %bitcast.14, ...), custom_call_target="tpu_custom_call" | custom-call | tf_op jit(solution)/shard_map/pallas_call | solution.py:438
  117.5 1.2 %copy.13 = f32[2,1,128]{2,1,0:T(1,128)} copy(f32[2,1,128]{2,1,0:T(1,128)} %bitcast.13) | data formatting | bytes 2048

commit v2 on v1

--- a/solution.py
+++ b/solution.py
@@ -15,7 +15,8 @@
 NY = 4
 NX = 4
 NZ = 8
-NCOL = NX * NZ * 2
+NCHIP = NX * NZ
+NCOL = NCHIP * 2
 EX = 6
 EA = 3
 TK = 4
@@ -23,6 +24,7 @@
 QD = D // 4
 CH = 256
 NCH = QD // CH
+MFIRST = 3
 SUB = CH // NY
 C = 128
 R1 = 64
@@ -57,12 +59,13 @@
 
 
 def kernel(
-    x_ref, og_ref, fm_ref, sm_ref, sin_ref, sout_ref, rin_ref, rout_ref, tid_ref, w_ref,
+    x_ref, og_ref, fm_ref, sm_ref, sin_hbm, sout_hbm, rin_hbm, rout_hbm, tid_hbm, w_hbm,
     out_ref,
-    rx, xs, xg, ogb, ogt, fmb, smb, ta, tb, left_s, right_s, hacc, sk, rs, qs, qr, ts, yr,
+    sin_ref, sout_ref, rin_ref, rout_ref, tid_ref, w_ref, s_small,
+    rx, xs, xg, ogb, ogt, fmb, smb, ta, tb, left_s, right_s, hacc, sk, sc, rs, qs, qr, ts, yr,
     s_rx, s_rxs, s_ogl, s_og, s_ogs, s_ml, s_mc, s_mcs, s_mx, s_mxs, s_my, s_mys,
     s_ax, s_axs, s_az, s_azs, s_bz, s_bzs, s_bx, s_bxs,
-    s_rs, s_rss, s_q, s_qs, s_t, s_tss,
+    s_sc, s_scs, s_rs, s_rss, s_q, s_qs, s_t, s_tss,
 ):
     y = lax.axis_index("grp")
     me = lax.axis_index("col")
@@ -97,13 +100,8 @@
         )
 
     barrier = pltpu.get_barrier_semaphore()
-
-    @pl.loop(1, NCOL)
-    def _(k):
-        pl.semaphore_signal(barrier, inc=1, device_id=(y, lax.rem(me + k, NCOL)), device_id_type=MESH)
-
-    for k in range(1, NY):
-        pl.semaphore_signal(barrier, inc=1, device_id=(lax.rem(y + k, NY), me), device_id_type=MESH)
+    for dev in (d_core, *d_xp, d_cross, *d_z, *d_y):
+        pl.semaphore_signal(barrier, inc=1, device_id=dev, device_id_type=MESH)
 
     og_local = []
     for p_ in range(2):
@@ -111,52 +109,33 @@
             cp = pltpu.make_async_copy(og_ref.at[:, p_, l_], ogb.at[blk, :, p_, :, l_], s_ogl.at[2 * p_ + l_])
             cp.start()
             og_local.append(cp)
-    x_local = pltpu.make_async_copy(x_ref.at[:, :, pl.ds(pl.multiple_of(quarter * QD, QD), QD)], rx.at[blk], s_rx.at[blk])
-    x_local.start()
-    pl.semaphore_wait(barrier, NCOL - 1 + NY - 1)
-
-    def x_send(dev, q, i):
-        return remote(x_ref.at[:, :, pl.ds(pl.multiple_of(q * QD, QD), QD)], rx.at[blk], s_rxs.at[i], s_rx.at[blk], dev)
-
-    x_sends = [
-        x_send(d_xp[0], 2 * (1 - cls), 0),
-        x_send(d_xp[1], 2 * (1 - cls) + 1, 1),
-        x_send(d_core, 2 * cls + 1 - core, 2),
-    ]
-    for cp in x_sends:
-        cp.start()
-    for cp in og_local:
-        cp.wait()
-    og_core = remote(ogb.at[blk], ogb.at[blk], s_ogs.at[0], s_og.at[0], d_core)
-    og_xp = remote(ogb.at[blk], ogb.at[blk], s_ogs.at[1], s_og.at[1], d_xsame)
-    og_xp.start()
-    og_core.start()
-
-    rows_in = as_column(rin_ref[...].astype(F32), R1).astype(jnp.int32)
-    rows_out = as_column(rout_ref[...].astype(F32), R2).astype(jnp.int32)
+    def x_part(q, j):
+        return x_ref.at[:, :, pl.ds(pl.multiple_of(q * QD + j * CH, CH), CH)]
+
+    def x_local(j):
+        return pltpu.make_async_copy(x_part(quarter, j), rx.at[j, blk], s_rx.at[j, blk])
+
+    def x_sends(j):
+        targets = ((d_xp[0], 2 * (1 - cls)), (d_xp[1], 2 * (1 - cls) + 1), (d_core, 2 * cls + 1 - core))
+        return [remote(x_part(q, j), rx.at[j, blk], s_rxs.at[j, i], s_rx.at[j, blk], dev) for i, (dev, q) in enumerate(targets)]
 
     @pl.loop(0, NCH)
     def _(j):
-        tile = quarter * NCH + j
-        cols = lax.broadcasted_iota(jnp.int32, (R1, CH), 1) + tile * CH
-        bit = jnp.bitwise_xor(parity(jnp.bitwise_and(rows_in, cols)), jnp.broadcast_to(sin_ref[tile], (R1, CH)))
-        left_s[j] = (1 - 2 * bit).astype(F32).astype(BF16)
-
-    for b in range(4):
-        owner = col(2 * pair + b // 2, z, b % 2)
-        cols = lax.broadcasted_iota(jnp.int32, (R2, C), 1) + owner * C
-        bit = jnp.bitwise_xor(parity(jnp.bitwise_and(rows_out, cols)), jnp.broadcast_to(sout_ref[owner], (R2, C)))
-        right_s[:, b * C:(b + 1) * C] = (1 - 2 * bit).astype(F32).astype(BF16)
-
-    hacc[...] = jnp.zeros_like(hacc)
-    sk[...] = jnp.zeros_like(sk)
-
-    for b in range(4):
-        pltpu.make_async_copy(rx.at[b], rx.at[b], s_rx.at[b]).wait()
-        xs[:, TK * b:TK * (b + 1), :] = rx[b].astype(F32)
-
-    for j in range(NCH):
-        xg[j, :, pair, z] = xs[:, :, j * CH:(j + 1) * CH].astype(BF16)
+        x_local(j).start()
+
+    small = []
+    for i, (src, dst) in enumerate(
+        ((sin_hbm, sin_ref), (sout_hbm, sout_ref), (rin_hbm, rin_ref), (rout_hbm, rout_ref), (tid_hbm, tid_ref), (w_hbm, w_ref))
+    ):
+        cp = pltpu.make_async_copy(src, dst, s_small.at[i])
+        cp.start()
+        small.append(cp)
+    pl.semaphore_wait(barrier, 8)
+
+    @pl.loop(0, NCH)
+    def _(j):
+        for cp in x_sends(j):
+            cp.start()
 
     A = slice(0, EA)
     B = slice(EA, EX)
@@ -167,8 +146,8 @@
     def zcome(s, up):
         return lax.rem(z + NZ - s, NZ) if up == 0 else lax.rem(z + s, NZ)
 
-    def a_x(j, where):
-        v = xg.at[j, A, where, z]
+    def own_x(j, where):
+        v = xg.at[j, :, where, z]
         return remote(v, v, s_axs.at[j], s_ax.at[j], d_cross)
 
     def a_z(j, s, up, zz):
@@ -179,9 +158,9 @@
         v = xg.at[j, B, pair, zz] if s < 4 else xg.at[j, B, pair, zz, :, pl.ds(up * HALF, HALF)]
         return remote(v, v, s_bzs.at[j, up, s - 1], s_bz.at[j, up, s - 1], d_z[up])
 
-    def b_x(j, where):
-        v = xg.at[j, B, where]
-        return remote(v, v, s_bxs.at[j], s_bx.at[j], d_cross)
+    def b_x(j, n, where, zz):
+        v = xg.at[j, B, where, zz]
+        return remote(v, v, s_bxs.at[j, n], s_bx.at[j, n], d_cross)
 
     moments = ((fm_ref, fmb), (sm_ref, smb))
 
@@ -213,6 +192,14 @@
 
     y2 = lax.rem(y + 2, NY)
 
+    def m_start(j):
+        for a in range(2):
+            for h in range(2):
+                m_x(j, a, h).start()
+        for a in range(2):
+            m_core(j, a, blk).start()
+            m_local(j, a).start()
+
     def stage(t, k, body):
         j = t - k
 
@@ -223,28 +210,29 @@
     def st5(j):
         for up in range(2):
             a_z(j, 4, up, zcome(4, up)).wait_recv()
-        b_x(j, 1 - pair).wait_recv()
 
     def st4(j):
         for up in range(2):
             b_z(j, 4, up, zcome(4, up)).wait_recv()
-        b_x(j, pair).start()
+        b_x(j, 6, pair, zcome(4, 0)).start()
         for up in range(2):
             a_z(j, 3, up, zcome(3, up)).wait_recv()
             a_z(j, 4, up, zback(4, up)).start()
 
+    def st_b(j, s):
+        for up in range(2):
+            b_z(j, s, up, zcome(s, up)).wait_recv()
+            b_z(j, s + 1, up, zback(s + 1, up)).start()
+            b_x(j, 2 * (s - 1) + up, pair, zcome(s, up)).start()
+
     def st3(j):
-        for up in range(2):
-            b_z(j, 3, up, zcome(3, up)).wait_recv()
-            b_z(j, 4, up, zback(4, up)).start()
+        st_b(j, 3)
         for up in range(2):
             a_z(j, 2, up, zcome(2, up)).wait_recv()
             a_z(j, 3, up, zback(3, up)).start()
 
     def st2(j):
-        for up in range(2):
-            b_z(j, 2, up, zcome(2, up)).wait_recv()
-            b_z(j, 3, up, zback(3, up)).start()
+        st_b(j, 2)
         for up in range(2):
             a_z(j, 1, up, zcome(1, up)).wait_recv()
             a_z(j, 2, up, zback(2, up)).start()
@@ -254,10 +242,8 @@
         m_y(j, 1, 2, yp, 1).start()
 
     def st1(j):
-        for up in range(2):
-            b_z(j, 1, up, zcome(1, up)).wait_recv()
-            b_z(j, 2, up, zback(2, up)).start()
-        a_x(j, 1 - pair).wait_recv()
+        st_b(j, 1)
+        own_x(j, 1 - pair).wait_recv()
         for up in range(2):
             a_z(j, 1, up, zback(1, up)).start()
         for a in range(2):
@@ -267,15 +253,13 @@
                 m_y(j, a, up, y, up).start()
 
     def st0(j):
-        a_x(j, pair).start()
+        for b in range(4):
+            pltpu.make_async_copy(rx.at[j, b], rx.at[j, b], s_rx.at[j, b]).wait()
+            xs[:, TK * b:TK * (b + 1), :] = rx[j, b].astype(F32)
+        xg[j, :, pair, z] = xs[...].astype(BF16)
+        own_x(j, pair).start()
         for up in range(2):
             b_z(j, 1, up, zback(1, up)).start()
-        for a in range(2):
-            for h in range(2):
-                m_x(j, a, h).start()
-        for a in range(2):
-            m_core(j, a, blk).start()
-            m_local(j, a).start()
 
     def compute(j):
         for a in range(2):
@@ -283,6 +267,9 @@
             m_y(j, a, 2, y2, a).wait_recv()
             m_core(j, a, 2 * low + 1 - core).wait_recv()
             m_local(j, a).wait()
+        for n in range(6):
+            b_x(j, n, 1 - pair, zcome(n // 2 + 1, n % 2)).wait_recv()
+        b_x(j, 6, 1 - pair, zcome(4, 0)).wait_recv()
         for b in range(4):
             ta[b * C:(b + 1) * C, :] = (fmb[j, b] * K_FM).T
             tb[b * C:(b + 1) * C, :] = (smb[j, b] * K_SM).T
@@ -317,6 +304,40 @@
                 v = ogb[b, e].astype(F32).reshape(4 * NZ * 8, C)
                 ogt[e, b * C:(b + 1) * C, :] = v.T.astype(BF16)
 
+    pl.loop(0, MFIRST)(m_start)
+    for cp in og_local:
+        cp.wait()
+    og_core = remote(ogb.at[blk], ogb.at[blk], s_ogs.at[0], s_og.at[0], d_core)
+    og_xp = remote(ogb.at[blk], ogb.at[blk], s_ogs.at[1], s_og.at[1], d_xsame)
+
+    og_xp.start()
+    og_core.start()
+    pl.loop(MFIRST, NCH)(m_start)
+
+    for cp in small:
+        cp.wait()
+    r = lax.broadcasted_iota(jnp.int32, (R1, R1), 0)
+    c = lax.broadcasted_iota(jnp.int32, (R1, R1), 1)
+    spread = jnp.where(2 * lax.rem(r, NCHIP) + r // NCHIP == c, jnp.broadcast_to(rin_ref[...].astype(F32), (R1, R1)), 0.0)
+    rows_in = jnp.sum(spread, axis=1, keepdims=True).astype(jnp.int32)
+    rows_out = as_column(rout_ref[...].astype(F32), R2).astype(jnp.int32)
+
+    @pl.loop(0, NCH)
+    def _(j):
+        tile = quarter * NCH + j
+        cols = lax.broadcasted_iota(jnp.int32, (R1, CH), 1) + tile * CH
+        bit = jnp.bitwise_xor(parity(jnp.bitwise_and(rows_in, cols)), jnp.broadcast_to(sin_ref[tile], (R1, CH)))
+        left_s[j] = (1 - 2 * bit).astype(F32).astype(BF16)
+
+    for b in range(4):
+        owner = col(2 * pair + b // 2, z, b % 2)
+        cols = lax.broadcasted_iota(jnp.int32, (R2, C), 1) + owner * C
+        bit = jnp.bitwise_xor(parity(jnp.bitwise_and(rows_out, cols)), jnp.broadcast_to(sout_ref[owner], (R2, C)))
+        right_s[:, b * C:(b + 1) * C] = (1 - 2 * bit).astype(F32).astype(BF16)
+
+    hacc[...] = jnp.zeros_like(hacc)
+    sk[...] = jnp.zeros_like(sk)
+
     @pl.loop(0, NCH + 5)
     def _(t):
         stage(t, 5, st5)
@@ -348,23 +369,32 @@
         part = part + lax.dot_general(hi, right_s[...], dims, preferred_element_type=F32)
         sk[:, e, :] = part
 
-    @pl.loop(1, NCOL)
-    def _(k):
-        to = lax.rem(me + k, NCOL)
-        remote(sk.at[to], rs.at[me], s_rss, s_rs, (y, to)).start()
-
-    rs[me] = sk[me]
-    some = rs.at[pl.ds(0, NCOL - 1)]
+    to_core = remote(
+        sk.at[pl.ds(pl.multiple_of((1 - core) * NCHIP, NCHIP), NCHIP)], sc, s_scs, s_sc, d_core
+    )
+    to_core.start()
+    hops = sorted(((min(i, NX - i) + min(k, NZ - k), i, k) for i in range(NX) for k in range(NZ)), reverse=True)
+    xt = [lax.rem(x + i, NX) * NZ for i in range(NX)]
+    zt = [lax.rem(z + i, NZ) for i in range(NZ)]
+    others = [xt[i] + zt[k] for _, i, k in hops if i or k]
+    chip = me // 2
+    to_core.wait()
+    sc[...] += sk[pl.ds(pl.multiple_of(core * NCHIP, NCHIP), NCHIP)]
+    for to in others:
+        remote(sc.at[to], rs.at[chip], s_rss, s_rs, (y, to * 2 + core)).start()
+
+    rs[chip] = sc[chip]
+    some = rs.at[pl.ds(0, NCHIP - 1)]
     remote(some, some, s_rss, s_rs, d_core).wait_recv()
     rows_sum = jnp.sum(rs[...], axis=0)
 
     sq = as_row(jnp.sum(rows_sum * rows_sum, axis=1, keepdims=True), C)
     qs[...] = sq
 
-    @pl.loop(1, NCOL)
-    def _(k):
-        to = lax.rem(me + k, NCOL)
-        remote(qs, qr.at[me], s_qs, s_q, (y, to)).start()
+    for to in others:
+        for c_ in (1 - core, core):
+            remote(qs, qr.at[me], s_qs, s_q, (y, to * 2 + c_)).start()
+    remote(qs, qr.at[me], s_qs, s_q, d_core).start()
 
     qr[me] = sq
     someq = qr.at[pl.ds(0, NCOL - 1)]
@@ -396,16 +426,18 @@
 
     remote(some, some, s_rss, s_rs, d_core).wait_send()
     remote(someq, someq, s_qs, s_q, d_core).wait_send()
-    for cp in x_sends:
-        cp.wait_send()
     og_core.wait_send()
     og_xp.wait_send()
     remote(ogb.at[2 * (1 - low) + core], ogb.at[2 * (1 - low) + core], s_ogs.at[2], s_og.at[2], d_core).wait_send()
 
     @pl.loop(0, NCH)
     def _(j):
-        a_x(j, pair).wait_send()
-        b_x(j, pair).wait_send()
+        for cp in x_sends(j):
+            cp.wait_send()
+        own_x(j, pair).wait_send()
+        for n in range(6):
+            b_x(j, n, pair, zcome(n // 2 + 1, n % 2)).wait_send()
+        b_x(j, 6, pair, zcome(4, 0)).wait_send()
         for up in range(2):
             for s in range(1, 5):
                 a_z(j, s, up, zback(s, up)).wait_send()
@@ -438,11 +470,18 @@
     out = pl.pallas_call(
         kernel,
         out_shape=jax.ShapeDtypeStruct((PRO, C), F32),
-        in_specs=[hbm] * 4 + [vmem] * 6,
+        in_specs=[hbm] * 10,
         out_specs=vmem,
         scratch_shapes=[
-            pltpu.VMEM((4, EX, TK, QD), BF16),
-            pltpu.VMEM((EX, 4 * TK, QD), F32),
+            pltpu.VMEM((D // CH, 1, CH), jnp.int32),
+            pltpu.VMEM((NCOL, 1, C), jnp.int32),
+            pltpu.VMEM((1, R1), jnp.int32),
+            pltpu.VMEM((1, R2), jnp.int32),
+            pltpu.VMEM((1, EX), jnp.int32),
+            pltpu.VMEM((1, EX), jnp.int32),
+            dma((6,)),
+            pltpu.VMEM((NCH, 4, EX, TK, CH), BF16),
+            pltpu.VMEM((EX, 4 * TK, CH), F32),
             pltpu.VMEM((NCH, EX, 2, NZ, 4 * TK, CH), BF16),
             pltpu.VMEM((4, EX, 2, NZ, 2, 8, C), BF16),
             pltpu.VMEM((EX, 4 * C, 256), BF16),
@@ -454,12 +493,13 @@
             pltpu.VMEM((R2, 4 * C), BF16),
             pltpu.VMEM((EX, R1, 4 * C), F32),
             pltpu.VMEM((NCOL, 8, C), F32),
-            pltpu.VMEM((NCOL, 8, C), F32),
+            pltpu.VMEM((NCHIP, 8, C), F32),
+            pltpu.VMEM((NCHIP, 8, C), F32),
             pltpu.VMEM((1, C), F32),
             pltpu.VMEM((NCOL, 1, C), F32),
             pltpu.VMEM((NY - 1, PRO, C), F32),
             pltpu.VMEM((NY - 1, PRO, C), F32),
-            dma((4,)), dma((3,)),
+            dma((NCH, 4)), dma((NCH, 3)),
             dma((4,)), dma((3,)), dma((3,)),
             dma((NCH, 2)),
             dma((NCH, 2)), dma((NCH, 2)),
@@ -468,8 +508,8 @@
             dma((NCH,)), dma((NCH,)),
             dma((NCH, 2, 4)), dma((NCH, 2, 4)),
             dma((NCH, 2, 4)), dma((NCH, 2, 4)),
-            dma((NCH,)), dma((NCH,)),
-            dma, dma, dma, dma,
+            dma((NCH, 7)), dma((NCH, 7)),
+            dma, dma, dma, dma, dma, dma,
             dma((NY - 1,)), dma((NY - 1,)),
         ],
         compiler_params=pltpu.CompilerParams(

time: 119 us -> 109 us (0.916)
  Pallas kernels: 117 us -> 108 us
    pallas_call x1, Pallas kernels: 117 us -> 108 us  [body(): pl.pallas_call(kernel, out_shape=jax.ShapeDtypeStruct((PRO, C), F32), in_...]
where the time goes in v2:
time: 109 us
  Pallas kernels  108 us (99%)
  local copies, waits for them, and re-layouts  1.24 us (1%)
    pallas_call x1, Pallas kernels, body(): pl.pallas_call(kernel, out_shape=jax.ShapeDtypeStruct((PRO, C), F32), in_...  108 us

profile of v2, /device:TPU:1, one launch (start us, length us, event | category | flops | bytes accessed | tf_op | source)
XLA Modules:
  0.0 109.0 jit_solution(10520427430564137124)
XLA Ops:
  0.0 107.8 %shard_map.100 = f32[2,128]{1,0:T(2,128)} custom-call(bf16[6,4,8192]{2,1,0:T(4,128)(2,1)} %x_ref.1, bf16[6,2,2,8,8,128]{5,4,3,2,1,0:T(8,128)(2,1)} %bitcast.10, f32[8192,128]{1,0:T(8,128)} %fm_ref.1, f32[8192,128]{1,0:T(8,128)} %sm_ref.1, s32[32,1,256]{2,1,0:T(1,128)} %bitcast.11, s32[64,1,128]{2,1,0:T(1,128)} %bitcast.12, s32[1,64]{1,0:T(1,128)} %bitcast.14, ...), custom_call_target="tpu_custom_call" | custom-call | tf_op jit(solution)/shard_map/pallas_call | solution.py:470
  107.8 1.2 %copy.13 = f32[2,1,128]{2,1,0:T(1,128)} copy(f32[2,1,128]{2,1,0:T(1,128)} %bitcast.13) | data formatting | bytes 2048

commit v3 on v2

--- a/solution.py
+++ b/solution.py
@@ -25,6 +25,9 @@
 CH = 256
 NCH = QD // CH
 MFIRST = 3
+Y_OWN = 2
+OG_ON = 4
+OG_END = 5
 SUB = CH // NY
 C = 128
 R1 = 64
@@ -207,59 +210,51 @@
         def _():
             body(j)
 
-    def st5(j):
-        for up in range(2):
-            a_z(j, 4, up, zcome(4, up)).wait_recv()
-
-    def st4(j):
-        for up in range(2):
-            b_z(j, 4, up, zcome(4, up)).wait_recv()
-        b_x(j, 6, pair, zcome(4, 0)).start()
-        for up in range(2):
-            a_z(j, 3, up, zcome(3, up)).wait_recv()
-            a_z(j, 4, up, zback(4, up)).start()
-
-    def st_b(j, s):
-        for up in range(2):
-            b_z(j, s, up, zcome(s, up)).wait_recv()
-            b_z(j, s + 1, up, zback(s + 1, up)).start()
-            b_x(j, 2 * (s - 1) + up, pair, zcome(s, up)).start()
-
-    def st3(j):
-        st_b(j, 3)
-        for up in range(2):
-            a_z(j, 2, up, zcome(2, up)).wait_recv()
-            a_z(j, 3, up, zback(3, up)).start()
-
-    def st2(j):
-        st_b(j, 2)
-        for up in range(2):
-            a_z(j, 1, up, zcome(1, up)).wait_recv()
-            a_z(j, 2, up, zback(2, up)).start()
-        m_y(j, 0, 0, ym, 0).wait_recv()
-        m_y(j, 0, 2, ym, 0).start()
-        m_y(j, 1, 1, yp, 1).wait_recv()
-        m_y(j, 1, 2, yp, 1).start()
-
-    def st1(j):
-        st_b(j, 1)
-        own_x(j, 1 - pair).wait_recv()
-        for up in range(2):
-            a_z(j, 1, up, zback(1, up)).start()
+    def a_step(s):
+        def go(j):
+            if s == 1:
+                own_x(j, 1 - pair).wait_recv()
+            for up in range(2):
+                if s > 1:
+                    a_z(j, s - 1, up, zcome(s - 1, up)).wait_recv()
+                if s < 5:
+                    a_z(j, s, up, zback(s, up)).start()
+
+        return go
+
+    def b_step(s):
+        def go(j):
+            for up in range(2):
+                if s > 1:
+                    b_z(j, s - 1, up, zcome(s - 1, up)).wait_recv()
+                if s < 5:
+                    b_z(j, s, up, zback(s, up)).start()
+                if 1 < s < 5:
+                    b_x(j, 2 * (s - 2) + up, pair, zcome(s - 1, up)).start()
+            if s == 5:
+                b_x(j, 6, pair, zcome(4, 0)).start()
+
+        return go
+
+    def own_piece(j):
+        for b in range(4):
+            pltpu.make_async_copy(rx.at[j, b], rx.at[j, b], s_rx.at[j, b]).wait()
+            xs[:, TK * b:TK * (b + 1), :] = rx[j, b].astype(F32)
+        xg[j, :, pair, z] = xs[...].astype(BF16)
+        own_x(j, pair).start()
+
+    def y_own(j):
         for a in range(2):
             for h in range(2):
                 m_x_come(j, a, h).wait_recv()
             for up in range(2):
                 m_y(j, a, up, y, up).start()
 
-    def st0(j):
-        for b in range(4):
-            pltpu.make_async_copy(rx.at[j, b], rx.at[j, b], s_rx.at[j, b]).wait()
-            xs[:, TK * b:TK * (b + 1), :] = rx[j, b].astype(F32)
-        xg[j, :, pair, z] = xs[...].astype(BF16)
-        own_x(j, pair).start()
-        for up in range(2):
-            b_z(j, 1, up, zback(1, up)).start()
+    def y_on(j):
+        m_y(j, 0, 0, ym, 0).wait_recv()
+        m_y(j, 0, 2, ym, 0).start()
+        m_y(j, 1, 1, yp, 1).wait_recv()
+        m_y(j, 1, 2, yp, 1).start()
 
     def compute(j):
         for a in range(2):
@@ -274,8 +269,7 @@
             ta[b * C:(b + 1) * C, :] = (fmb[j, b] * K_FM).T
             tb[b * C:(b + 1) * C, :] = (smb[j, b] * K_SM).T
 
-        @pl.loop(0, EX)
-        def _(e):
+        def one(e):
             acts = xg[j, e].reshape(2 * NZ * 4 * TK, CH)
             for h in range(2):
                 sl = slice(h * 2 * C, (h + 1) * 2 * C)
@@ -287,6 +281,9 @@
                     left_s[j], u, (((1,), (1,)), ((), ())), preferred_element_type=F32
                 )
 
+        for e in range(EX):
+            one(e)
+
     def og_forward():
         og_in = remote(ogb.at[2 * (1 - low) + core], ogb.at[2 * (1 - low) + core], s_ogs.at[1], s_og.at[1], d_xsame)
         og_in.wait_recv()
@@ -340,18 +337,19 @@
 
     @pl.loop(0, NCH + 5)
     def _(t):
-        stage(t, 5, st5)
-        stage(t, 4, st4)
-        stage(t, 3, st3)
-        stage(t, 2, st2)
-        stage(t, 1, st1)
-        stage(t, 0, st0)
-
-        @pl.when(t == 2)
+        for s in (5, 4, 3, 2, 1):
+            stage(t, s, a_step(s))
+        stage(t, 0, own_piece)
+        stage(t, Y_OWN, y_own)
+        for s in (5, 4, 3, 2, 1):
+            stage(t, s - 1, b_step(s))
+        stage(t, Y_OWN + 1, y_on)
+
+        @pl.when(t == OG_ON)
         def _():
             og_forward()
 
-        @pl.when(t == 4)
+        @pl.when(t == OG_END)
         def _():
             og_finish()
 

time: 109 us -> 94.6 us (0.87)
  Pallas kernels: 108 us -> 93.3 us
    pallas_call x1, Pallas kernels: 108 us -> 93.3 us  [body(): pl.pallas_call(kernel, out_shape=jax.ShapeDtypeStruct((PRO, C), F32), in_...]
where the time goes in v3:
time: 94.6 us; the launch traced here: 94.5 us
  Pallas kernels  93.3 us (99%)
  local copies, waits for them, and re-layouts  1.24 us (1%)
    pallas_call x1, Pallas kernels, body(): pl.pallas_call(kernel, out_shape=jax.ShapeDtypeStruct((PRO, C), F32), in_...  93.3 us

profile of v3, /device:TPU:1, one launch (start us, length us, event | category | flops | bytes accessed | tf_op | source)
XLA Modules:
  0.0 94.5 jit_solution(4234541398583366340)
XLA Ops:
  0.0 93.3 %shard_map.100 = f32[2,128]{1,0:T(2,128)} custom-call(bf16[6,4,8192]{2,1,0:T(4,128)(2,1)} %x_ref.1, bf16[6,2,2,8,8,128]{5,4,3,2,1,0:T(8,128)(2,1)} %bitcast.10, f32[8192,128]{1,0:T(8,128)} %fm_ref.1, f32[8192,128]{1,0:T(8,128)} %sm_ref.1, s32[32,1,256]{2,1,0:T(1,128)} %bitcast.11, s32[64,1,128]{2,1,0:T(1,128)} %bitcast.12, s32[1,64]{1,0:T(1,128)} %bitcast.14, ...), custom_call_target="tpu_custom_call" | custom-call | tf_op jit(solution)/shard_map/pallas_call | solution.py:468
  93.3 1.2 %copy.13 = f32[2,1,128]{2,1,0:T(1,128)} copy(f32[2,1,128]{2,1,0:T(1,128)} %bitcast.13) | data formatting | bytes 2048

commit v4 on v3

--- a/solution.py
+++ b/solution.py
@@ -18,13 +18,14 @@
 NCHIP = NX * NZ
 NCOL = NCHIP * 2
 EX = 6
-EA = 3
 TK = 4
 D = 8192
 QD = D // 4
 CH = 256
 NCH = QD // CH
-MFIRST = 3
+MFIRST = 6
+EA = (3, 2, 3, 2, 3, 2, 3, 2)
+FIRST = (0, 0, 1, 1, 2, 2, 3, 3)
 Y_OWN = 2
 OG_ON = 4
 OG_END = 5
@@ -140,8 +141,11 @@
         for cp in x_sends(j):
             cp.start()
 
-    A = slice(0, EA)
-    B = slice(EA, EX)
+    def A(j):
+        return slice(0, EA[j])
+
+    def B(j):
+        return slice(EA[j], EX)
 
     def zback(s, up):
         return lax.rem(z + NZ - (s - 1), NZ) if up == 0 else lax.rem(z + s - 1, NZ)
@@ -154,15 +158,15 @@
         return remote(v, v, s_axs.at[j], s_ax.at[j], d_cross)
 
     def a_z(j, s, up, zz):
-        v = xg.at[j, A, :, zz] if s < 4 else xg.at[j, A, :, zz, :, pl.ds(up * HALF, HALF)]
+        v = xg.at[j, A(j), :, zz] if s < 4 else xg.at[j, A(j), :, zz, :, pl.ds(up * HALF, HALF)]
         return remote(v, v, s_azs.at[j, up, s - 1], s_az.at[j, up, s - 1], d_z[up])
 
     def b_z(j, s, up, zz):
-        v = xg.at[j, B, pair, zz] if s < 4 else xg.at[j, B, pair, zz, :, pl.ds(up * HALF, HALF)]
+        v = xg.at[j, B(j), pair, zz] if s < 4 else xg.at[j, B(j), pair, zz, :, pl.ds(up * HALF, HALF)]
         return remote(v, v, s_bzs.at[j, up, s - 1], s_bz.at[j, up, s - 1], d_z[up])
 
     def b_x(j, n, where, zz):
-        v = xg.at[j, B, where, zz]
+        v = xg.at[j, B(j), where, zz]
         return remote(v, v, s_bxs.at[j, n], s_bx.at[j, n], d_cross)
 
     moments = ((fm_ref, fmb), (sm_ref, smb))
@@ -202,13 +206,6 @@
         for a in range(2):
             m_core(j, a, blk).start()
             m_local(j, a).start()
-
-    def stage(t, k, body):
-        j = t - k
-
-        @pl.when(jnp.logical_and(j >= 0, j < NCH))
-        def _():
-            body(j)
 
     def a_step(s):
         def go(j):
@@ -335,25 +332,24 @@
     hacc[...] = jnp.zeros_like(hacc)
     sk[...] = jnp.zeros_like(sk)
 
-    @pl.loop(0, NCH + 5)
-    def _(t):
+    for t in range(FIRST[-1] + 6):
+        def stage(step, body):
+            for j in range(NCH):
+                if FIRST[j] + step == t:
+                    body(j)
+
         for s in (5, 4, 3, 2, 1):
-            stage(t, s, a_step(s))
-        stage(t, 0, own_piece)
-        stage(t, Y_OWN, y_own)
+            stage(s, a_step(s))
+        stage(0, own_piece)
+        stage(Y_OWN, y_own)
         for s in (5, 4, 3, 2, 1):
-            stage(t, s - 1, b_step(s))
-        stage(t, Y_OWN + 1, y_on)
-
-        @pl.when(t == OG_ON)
-        def _():
+            stage(s - 1, b_step(s))
+        stage(Y_OWN + 1, y_on)
+        if t == OG_ON:
             og_forward()
-
-        @pl.when(t == OG_END)
-        def _():
+        if t == OG_END:
             og_finish()
-
-        stage(t, 5, compute)
+        stage(5, compute)
 
     for e in range(EX):
         h = hacc[e]
@@ -428,8 +424,7 @@
     og_xp.wait_send()
     remote(ogb.at[2 * (1 - low) + core], ogb.at[2 * (1 - low) + core], s_ogs.at[2], s_og.at[2], d_core).wait_send()
 
-    @pl.loop(0, NCH)
-    def _(j):
+    for j in range(NCH):
         for cp in x_sends(j):
             cp.wait_send()
         own_x(j, pair).wait_send()

time: 94.6 us -> 89.8 us (0.949)
  Pallas kernels: 93.3 us -> 88.4 us
    pallas_call x1, Pallas kernels: 93.3 us -> 88.4 us  [body(): pl.pallas_call(kernel, out_shape=jax.ShapeDtypeStruct((PRO, C), F32), in_...]
where the time goes in v4:
time: 89.8 us; the launch traced here: 89.7 us
  Pallas kernels  88.4 us (98%)
  local copies, waits for them, and re-layouts  1.24 us (1%)
    pallas_call x1, Pallas kernels, body(): pl.pallas_call(kernel, out_shape=jax.ShapeDtypeStruct((PRO, C), F32), in_...  88.4 us

profile of v4, /device:TPU:1, one launch (start us, length us, event | category | flops | bytes accessed | tf_op | source)
XLA Modules:
  0.0 89.7 jit_solution(3186119678593536904)
XLA Ops:
  0.0 88.4 %shard_map.100 = f32[2,128]{1,0:T(2,128)} custom-call(bf16[6,4,8192]{2,1,0:T(4,128)(2,1)} %x_ref.1, bf16[6,2,2,8,8,128]{5,4,3,2,1,0:T(8,128)(2,1)} %bitcast.10, f32[8192,128]{1,0:T(8,128)} %fm_ref.1, f32[8192,128]{1,0:T(8,128)} %sm_ref.1, s32[32,1,256]{2,1,0:T(1,128)} %bitcast.11, s32[64,1,128]{2,1,0:T(1,128)} %bitcast.12, s32[1,64]{1,0:T(1,128)} %bitcast.14, ...), custom_call_target="tpu_custom_call" | custom-call | tf_op jit(solution)/shard_map/pallas_call | solution.py:463
  88.4 1.2 %copy.13 = f32[2,1,128]{2,1,0:T(1,128)} copy(f32[2,1,128]{2,1,0:T(1,128)} %bitcast.13) | data formatting | bytes 2048

commit v5 on v4

--- a/solution.py
+++ b/solution.py
@@ -23,7 +23,7 @@
 QD = D // 4
 CH = 256
 NCH = QD // CH
-MFIRST = 6
+MFIRST = 8
 EA = (3, 2, 3, 2, 3, 2, 3, 2)
 FIRST = (0, 0, 1, 1, 2, 2, 3, 3)
 Y_OWN = 2
@@ -298,40 +298,6 @@
                 v = ogb[b, e].astype(F32).reshape(4 * NZ * 8, C)
                 ogt[e, b * C:(b + 1) * C, :] = v.T.astype(BF16)
 
-    pl.loop(0, MFIRST)(m_start)
-    for cp in og_local:
-        cp.wait()
-    og_core = remote(ogb.at[blk], ogb.at[blk], s_ogs.at[0], s_og.at[0], d_core)
-    og_xp = remote(ogb.at[blk], ogb.at[blk], s_ogs.at[1], s_og.at[1], d_xsame)
-
-    og_xp.start()
-    og_core.start()
-    pl.loop(MFIRST, NCH)(m_start)
-
-    for cp in small:
-        cp.wait()
-    r = lax.broadcasted_iota(jnp.int32, (R1, R1), 0)
-    c = lax.broadcasted_iota(jnp.int32, (R1, R1), 1)
-    spread = jnp.where(2 * lax.rem(r, NCHIP) + r // NCHIP == c, jnp.broadcast_to(rin_ref[...].astype(F32), (R1, R1)), 0.0)
-    rows_in = jnp.sum(spread, axis=1, keepdims=True).astype(jnp.int32)
-    rows_out = as_column(rout_ref[...].astype(F32), R2).astype(jnp.int32)
-
-    @pl.loop(0, NCH)
-    def _(j):
-        tile = quarter * NCH + j
-        cols = lax.broadcasted_iota(jnp.int32, (R1, CH), 1) + tile * CH
-        bit = jnp.bitwise_xor(parity(jnp.bitwise_and(rows_in, cols)), jnp.broadcast_to(sin_ref[tile], (R1, CH)))
-        left_s[j] = (1 - 2 * bit).astype(F32).astype(BF16)
-
-    for b in range(4):
-        owner = col(2 * pair + b // 2, z, b % 2)
-        cols = lax.broadcasted_iota(jnp.int32, (R2, C), 1) + owner * C
-        bit = jnp.bitwise_xor(parity(jnp.bitwise_and(rows_out, cols)), jnp.broadcast_to(sout_ref[owner], (R2, C)))
-        right_s[:, b * C:(b + 1) * C] = (1 - 2 * bit).astype(F32).astype(BF16)
-
-    hacc[...] = jnp.zeros_like(hacc)
-    sk[...] = jnp.zeros_like(sk)
-
     for t in range(FIRST[-1] + 6):
         def stage(step, body):
             for j in range(NCH):
@@ -345,6 +311,42 @@
         for s in (5, 4, 3, 2, 1):
             stage(s - 1, b_step(s))
         stage(Y_OWN + 1, y_on)
+        if t == 0:
+            pl.loop(0, MFIRST)(m_start)
+            for cp in og_local:
+                cp.wait()
+            og_core = remote(ogb.at[blk], ogb.at[blk], s_ogs.at[0], s_og.at[0], d_core)
+            og_xp = remote(ogb.at[blk], ogb.at[blk], s_ogs.at[1], s_og.at[1], d_xsame)
+
+            og_xp.start()
+            og_core.start()
+            pl.loop(MFIRST, NCH)(m_start)
+
+        if t == 1:
+            for cp in small:
+                cp.wait()
+            r = lax.broadcasted_iota(jnp.int32, (R1, R1), 0)
+            c = lax.broadcasted_iota(jnp.int32, (R1, R1), 1)
+            spread = jnp.where(2 * lax.rem(r, NCHIP) + r // NCHIP == c, jnp.broadcast_to(rin_ref[...].astype(F32), (R1, R1)), 0.0)
+            rows_in = jnp.sum(spread, axis=1, keepdims=True).astype(jnp.int32)
+            rows_out = as_column(rout_ref[...].astype(F32), R2).astype(jnp.int32)
+
+            @pl.loop(0, NCH)
+            def _(j):
+                tile = quarter * NCH + j
+                cols = lax.broadcasted_iota(jnp.int32, (R1, CH), 1) + tile * CH
+                bit = jnp.bitwise_xor(parity(jnp.bitwise_and(rows_in, cols)), jnp.broadcast_to(sin_ref[tile], (R1, CH)))
+                left_s[j] = (1 - 2 * bit).astype(F32).astype(BF16)
+
+            for b in range(4):
+                owner = col(2 * pair + b // 2, z, b % 2)
+                cols = lax.broadcasted_iota(jnp.int32, (R2, C), 1) + owner * C
+                bit = jnp.bitwise_xor(parity(jnp.bitwise_and(rows_out, cols)), jnp.broadcast_to(sout_ref[owner], (R2, C)))
+                right_s[:, b * C:(b + 1) * C] = (1 - 2 * bit).astype(F32).astype(BF16)
+
+            hacc[...] = jnp.zeros_like(hacc)
+            sk[...] = jnp.zeros_like(sk)
+
         if t == OG_ON:
             og_forward()
         if t == OG_END:
@@ -378,48 +380,9 @@
         remote(sc.at[to], rs.at[chip], s_rss, s_rs, (y, to * 2 + core)).start()
 
     rs[chip] = sc[chip]
-    some = rs.at[pl.ds(0, NCHIP - 1)]
-    remote(some, some, s_rss, s_rs, d_core).wait_recv()
-    rows_sum = jnp.sum(rs[...], axis=0)
-
-    sq = as_row(jnp.sum(rows_sum * rows_sum, axis=1, keepdims=True), C)
-    qs[...] = sq
-
-    for to in others:
-        for c_ in (1 - core, core):
-            remote(qs, qr.at[me], s_qs, s_q, (y, to * 2 + c_)).start()
-    remote(qs, qr.at[me], s_qs, s_q, d_core).start()
-
-    qr[me] = sq
-    someq = qr.at[pl.ds(0, NCOL - 1)]
-    remote(someq, someq, s_qs, s_q, d_core).wait_recv()
-    squares = as_column(jnp.sum(qr[...], axis=0), 8)
-    unit = rows_sum * lax.rsqrt(squares / (R1 * R2) + 1e-06)
-
     tid = as_column(tid_ref[...].astype(F32), 8)
     wgt = as_column(w_ref[...].astype(F32), 8)
 
-    def term(p):
-        coef = jnp.where(tid == p.astype(F32), wgt, 0.0)
-        return jnp.sum(coef * unit, axis=0, keepdims=True)
-
-    def terms(g):
-        return jnp.concatenate([term(PRO * g + i) for i in range(PRO)], axis=0)
-
-    y_sends = []
-    for k in range(1, NY):
-        g = lax.rem(y + k, NY)
-        ts[k - 1] = terms(g)
-        cp = remote(ts.at[k - 1], yr.at[k - 1], s_tss.at[k - 1], s_t.at[k - 1], (g, me))
-        cp.start()
-        y_sends.append(cp)
-    total = terms(y)
-    for cp in y_sends:
-        cp.wait()
-    out_ref[...] = total + (yr[0] + yr[1] + yr[2])
-
-    remote(some, some, s_rss, s_rs, d_core).wait_send()
-    remote(someq, someq, s_qs, s_q, d_core).wait_send()
     og_core.wait_send()
     og_xp.wait_send()
     remote(ogb.at[2 * (1 - low) + core], ogb.at[2 * (1 - low) + core], s_ogs.at[2], s_og.at[2], d_core).wait_send()
@@ -443,6 +406,47 @@
                 m_y(j, a, up, y, up).wait_send()
         m_y(j, 0, 2, ym, 0).wait_send()
         m_y(j, 1, 2, yp, 1).wait_send()
+
+    some = rs.at[pl.ds(0, NCHIP - 1)]
+    remote(some, some, s_rss, s_rs, d_core).wait_recv()
+    rows_sum = jnp.sum(rs[...], axis=0)
+
+    sq = as_row(jnp.sum(rows_sum * rows_sum, axis=1, keepdims=True), C)
+    qs[...] = sq
+
+    for to in others:
+        for c_ in (1 - core, core):
+            remote(qs, qr.at[me], s_qs, s_q, (y, to * 2 + c_)).start()
+    remote(qs, qr.at[me], s_qs, s_q, d_core).start()
+
+    qr[me] = sq
+    someq = qr.at[pl.ds(0, NCOL - 1)]
+    remote(someq, someq, s_qs, s_q, d_core).wait_recv()
+    squares = as_column(jnp.sum(qr[...], axis=0), 8)
+    unit = rows_sum * lax.rsqrt(squares / (R1 * R2) + 1e-06)
+
+
+    def term(p):
+        coef = jnp.where(tid == p.astype(F32), wgt, 0.0)
+        return jnp.sum(coef * unit, axis=0, keepdims=True)
+
+    def terms(g):
+        return jnp.concatenate([term(PRO * g + i) for i in range(PRO)], axis=0)
+
+    y_sends = []
+    for k in range(1, NY):
+        g = lax.rem(y + k, NY)
+        ts[k - 1] = terms(g)
+        cp = remote(ts.at[k - 1], yr.at[k - 1], s_tss.at[k - 1], s_t.at[k - 1], (g, me))
+        cp.start()
+        y_sends.append(cp)
+    total = terms(y)
+    for cp in y_sends:
+        cp.wait()
+    out_ref[...] = total + (yr[0] + yr[1] + yr[2])
+
+    remote(some, some, s_rss, s_rs, d_core).wait_send()
+    remote(someq, someq, s_qs, s_q, d_core).wait_send()
 
 
 def body(

time: 89.8 us -> 89.3 us (level)
  no operation moved by 1% of the time
where the time goes in v5:
time: 89.3 us; the launch traced here: 89.2 us
  Pallas kernels  87.9 us (98%)
  local copies, waits for them, and re-layouts  1.24 us (1%)
    pallas_call x1, Pallas kernels, body(): pl.pallas_call(kernel, out_shape=jax.ShapeDtypeStruct((PRO, C), F32), in_...  87.9 us

profile of v5, /device:TPU:1, one launch (start us, length us, event | category | flops | bytes accessed | tf_op | source)
XLA Modules:
  0.0 89.2 jit_solution(11505167636382880351)
XLA Ops:
  0.0 87.9 %shard_map.100 = f32[2,128]{1,0:T(2,128)} custom-call(bf16[6,4,8192]{2,1,0:T(4,128)(2,1)} %x_ref.1, bf16[6,2,2,8,8,128]{5,4,3,2,1,0:T(8,128)(2,1)} %bitcast.10, f32[8192,128]{1,0:T(8,128)} %fm_ref.1, f32[8192,128]{1,0:T(8,128)} %sm_ref.1, s32[32,1,256]{2,1,0:T(1,128)} %bitcast.11, s32[64,1,128]{2,1,0:T(1,128)} %bitcast.12, s32[1,64]{1,0:T(1,128)} %bitcast.14, ...), custom_call_target="tpu_custom_call" | custom-call | tf_op jit(solution)/shard_map/pallas_call | solution.py:467
  87.9 1.2 %copy.13 = f32[2,1,128]{2,1,0:T(1,128)} copy(f32[2,1,128]{2,1,0:T(1,128)} %bitcast.13) | data formatting | bytes 2048

commit v6 on v5

--- a/solution.py
+++ b/solution.py
@@ -307,10 +307,10 @@
         for s in (5, 4, 3, 2, 1):
             stage(s, a_step(s))
         stage(0, own_piece)
-        stage(Y_OWN, y_own)
         for s in (5, 4, 3, 2, 1):
             stage(s - 1, b_step(s))
         stage(Y_OWN + 1, y_on)
+        stage(Y_OWN, y_own)
         if t == 0:
             pl.loop(0, MFIRST)(m_start)
             for cp in og_local:

time: 89.3 us -> 94.1 us (1.054)
  Pallas kernels: 87.9 us -> 92.8 us
    pallas_call x1, Pallas kernels: 87.9 us -> 92.8 us  [body(): pl.pallas_call(kernel, out_shape=jax.ShapeDtypeStruct((PRO, C), F32), in_...]
where the time goes in v6:
time: 94.1 us; the launch traced here: 94 us
  Pallas kernels  92.8 us (99%)
  local copies, waits for them, and re-layouts  1.24 us (1%)
    pallas_call x1, Pallas kernels, body(): pl.pallas_call(kernel, out_shape=jax.ShapeDtypeStruct((PRO, C), F32), in_...  92.8 us

profile of v6, /device:TPU:1, one launch (start us, length us, event | category | flops | bytes accessed | tf_op | source)
XLA Modules:
  0.0 94.0 jit_solution(7177110350242087281)
XLA Ops:
  0.0 92.8 %shard_map.100 = f32[2,128]{1,0:T(2,128)} custom-call(bf16[6,4,8192]{2,1,0:T(4,128)(2,1)} %x_ref.1, bf16[6,2,2,8,8,128]{5,4,3,2,1,0:T(8,128)(2,1)} %bitcast.10, f32[8192,128]{1,0:T(8,128)} %fm_ref.1, f32[8192,128]{1,0:T(8,128)} %sm_ref.1, s32[32,1,256]{2,1,0:T(1,128)} %bitcast.11, s32[64,1,128]{2,1,0:T(1,128)} %bitcast.12, s32[1,64]{1,0:T(1,128)} %bitcast.14, ...), custom_call_target="tpu_custom_call" | custom-call | tf_op jit(solution)/shard_map/pallas_call | solution.py:467
  92.8 1.2 %copy.13 = f32[2,1,128]{2,1,0:T(1,128)} copy(f32[2,1,128]{2,1,0:T(1,128)} %bitcast.13) | data formatting | bytes 2048
